TPU v7x, 32 devices: a whole 2x2x4 slice. The times are simulated.
32 devices in a mesh: elem: 16 (over z, x, core), head: 2 (over y).
Axes of the slice: x: 2, y: 2, z: 4, core: 2. Of those that a mesh axis runs over, the one named last changes fastest.
Arguments:
- features: bfloat16 [16384, 512], P('elem'), may hold values from -6 to 6
- out_grad: bfloat16 [16384, 512], P('elem'), may hold values from -6 to 6
- bin_order: int32 [16384], P('elem'), may hold values from 0 to 16383, as said below
- key_lists: int32 [128, 12], P('elem'), may hold values from 0 to 127, as said below
- list_counts: int32 [128], P('elem'), may hold values from 1 to 12, as said below
- attn_gain: float32 [512], replicated, may hold values from 0.1 to 1.9
- query_weight: bfloat16 [512, 512], P(None, 'head')
- key_weight: bfloat16 [512, 512], P(None, 'head')
- value_weight: bfloat16 [512, 512], P(None, 'head'), may hold values from -0.25 to 0.25
- out_weight: bfloat16 [512, 512], P('head'), may hold values from -0.25 to 0.25
- ffn_gain: float32 [512], replicated, may hold values from 0.1 to 1.9
- ffn_in: bfloat16 [512, 2048], P(None, 'head'), may hold values from -0.25 to 0.25
- ffn_out: bfloat16 [2048, 512], P('head'), may hold values from -0.125 to 0.125
Outputs:
- output: bfloat16 [16384, 512], P('elem', 'head')
- input_grad: float32 [16384, 512], P('elem', 'head')
Inputs may be any that keep to these rules, and one draw needn't show every extreme that they name: `bin_order`: the rows of region e, numbers e * 1024 to (e + 1) * 1024 - 1, hold a permutation of those same numbers. `key_lists`: slot 0 of row b is b; the other slots hold distinct blocks other than b, all of the regions r - 1, r and r + 1 modulo 16, where r = b // 8 and region r holds blocks r * 8 to (r + 1) * 8 - 1; in row r * 8 of every region, slot 1 is a block of region r - 1 and slot 2 a block of region r + 1. list_counts[r * 8] = 12 for every region r.
All inputs are finite; a program needn't handle non-finite values.
Results may differ from a plain program's by a relative error of at most 0.024.
Values may be sent and summed in bfloat16 or wider, within the bound.
No kernel may reach another device: no remote copies, remote signals or barrier semaphores. Data moves between devices by JAX's collectives and lax.ppermute only.
A program may use at most 128 MiB of HBM per device.

v0:
```python
import jax
import jax.numpy as jnp
from jax import lax
from jax.sharding import PartitionSpec as P

HD = 64
EPSILON = 1e-05


def padded(block, sides, width):
    for axis, dim in sides:
        count = lax.axis_size(axis)
        forward = [(i, i + 1) for i in range(count - 1)]
        forward.append((count - 1, 0))
        backward = [(target, source) for source, target in forward]
        low = lax.ppermute(
            lax.slice_in_dim(block, block.shape[dim] - width, None, axis=dim), axis, forward
        )
        high = lax.ppermute(lax.slice_in_dim(block, 0, width, axis=dim), axis, backward)
        block = jnp.concatenate([low, block, high], axis=dim)
    return block


def from_behind(value, axis, steps):
    count = lax.axis_size(axis)
    pairs = [(source, (source + steps) % count) for source in range(count)]
    return lax.ppermute(value, axis, pairs)


def row_scale(values):
    return lax.rsqrt(jnp.mean(values * values, axis=-1, keepdims=True) + EPSILON)


def local(
    features,
    out_grad,
    bin_order,
    key_lists,
    list_counts,
    attn_gain,
    query_weight,
    key_weight,
    value_weight,
    out_weight,
    ffn_gain,
    ffn_in,
    ffn_out,
):
    row_count, model_width = features.shape
    block_count = key_lists.shape[0]
    block_len = row_count // block_count
    col_share = query_weight.shape[1]
    local_heads = col_share // HD
    scale_for_scores = HD ** (-0.5)
    highest_precision = lax.Precision.HIGHEST
    region = lax.axis_index("elem")
    regions = lax.axis_size("elem")
    head_group = lax.axis_index("head")
    col_start = head_group * col_share
    positions = bin_order - region * row_count
    owners = key_lists // block_count
    relative = jnp.mod(owners - region + 1, regions)
    buffer_index = relative * block_count + key_lists % block_count
    top_count = jnp.max(list_counts)
    wide_blocks = 3 * block_count
    block_ids = jnp.arange(wide_blocks, dtype=jnp.int32)
    ordered_rows = jnp.take(features, positions, axis=0).astype(jnp.float32)
    first_scale = row_scale(ordered_rows)
    first_norm = ordered_rows * first_scale
    normed = (first_norm * attn_gain).astype(jnp.bfloat16)
    queries = jnp.dot(normed, query_weight, preferred_element_type=jnp.float32).astype(jnp.bfloat16)
    pair_weights = jnp.concatenate([key_weight, value_weight], axis=1)
    widened = padded(normed, (("elem", 0),), row_count)
    pair_rows = jnp.dot(widened, pair_weights, preferred_element_type=jnp.float32).astype(
        jnp.bfloat16
    )
    wide_rows = 3 * row_count
    pair_blocks = pair_rows.reshape(wide_blocks, block_len, 2 * col_share)
    query_blocks = queries.reshape(block_count, block_len, local_heads, HD)

    def slot_table(slot_pos):
        picked = lax.dynamic_index_in_dim(buffer_index, slot_pos, axis=1, keepdims=False)
        return picked[:, None] == block_ids[None, :]

    def slot_scores(slot_pos):
        table = slot_table(slot_pos)
        tiles = jnp.einsum(
            "bc,ckf->bkf",
            table.astype(jnp.bfloat16),
            pair_blocks,
            preferred_element_type=jnp.float32,
        ).astype(jnp.bfloat16)
        key_tile_blocks = tiles[:, :, :col_share].reshape(block_count, block_len, local_heads, HD)
        value_tile_blocks = tiles[:, :, col_share:].reshape(block_count, block_len, local_heads, HD)
        attention_scores = (
            jnp.einsum(
                "bqhd,bkhd->bhqk", query_blocks, key_tile_blocks, preferred_element_type=jnp.float32
            )
            * scale_for_scores
        )
        live_mask = (slot_pos < list_counts)[:, None, None, None]
        return (
            jnp.where(live_mask, attention_scores, -jnp.inf),
            table,
            key_tile_blocks,
            value_tile_blocks,
        )

    first_scores, first_table, first_keys, first_values = slot_scores(0)
    run_max = jnp.max(first_scores, axis=-1)
    run_total = jnp.sum(jnp.exp(first_scores - run_max[..., None]), axis=-1)

    def stats_step(slot_pos, carried):
        old_max, old_total = carried
        attention_scores, table, key_tile_blocks, value_tile_blocks = slot_scores(slot_pos)
        new_max = jnp.maximum(old_max, jnp.max(attention_scores, axis=-1))
        new_total = old_total * jnp.exp(old_max - new_max) + jnp.sum(
            jnp.exp(attention_scores - new_max[..., None]), axis=-1
        )
        return (new_max, new_total)

    run_max, run_total = lax.fori_loop(1, top_count, stats_step, (run_max, run_total))
    log_total = run_max + jnp.log(run_total)

    def output_step(slot_pos, running):
        attention_scores, table, key_tile_blocks, value_tile_blocks = slot_scores(slot_pos)
        attn_probs = jnp.exp(attention_scores - log_total[..., None]).astype(jnp.bfloat16)
        return running + jnp.einsum(
            "bhqk,bkhd->bqhd", attn_probs, value_tile_blocks, preferred_element_type=jnp.float32
        )

    attended_sum = lax.fori_loop(
        0, top_count, output_step, jnp.zeros((block_count, block_len, local_heads, HD), jnp.float32)
    )
    attended_output = attended_sum.reshape(row_count, col_share).astype(jnp.bfloat16)
    mixed_heads = lax.psum(
        jnp.dot(attended_output, out_weight, preferred_element_type=jnp.float32).astype(
            jnp.bfloat16
        ),
        "head",
    ).astype(jnp.float32)
    hidden_in = ordered_rows + mixed_heads
    second_scale = row_scale(hidden_in)
    second_norm = hidden_in * second_scale
    normed_two = (second_norm * ffn_gain).astype(jnp.bfloat16)
    pre_act = jnp.dot(normed_two, ffn_in, preferred_element_type=jnp.float32)
    activated = jax.nn.gelu(pre_act).astype(jnp.bfloat16)
    ffn_terms = jnp.dot(activated, ffn_out, preferred_element_type=jnp.float32)
    ffn_total = lax.psum(ffn_terms.astype(jnp.bfloat16), "head").astype(jnp.float32)
    out_sorted = lax.dynamic_slice_in_dim(hidden_in + ffn_total, col_start, col_share, 1).astype(
        jnp.bfloat16
    )
    grad_sorted = jnp.take(out_grad, positions, axis=0)
    grad_act = jnp.dot(grad_sorted, ffn_out.T, preferred_element_type=jnp.float32)
    gelu_value, gelu_pull = jax.vjp(jax.nn.gelu, pre_act)
    grad_pre = gelu_pull(grad_act)[0].astype(jnp.bfloat16)
    norm_grad = lax.psum(
        jnp.dot(grad_pre, ffn_in.T, preferred_element_type=jnp.float32).astype(jnp.bfloat16), "head"
    ).astype(jnp.float32)
    scaled_grad = norm_grad * ffn_gain
    grad_hidden = grad_sorted.astype(jnp.float32) + second_scale * (
        scaled_grad - second_norm * jnp.mean(scaled_grad * second_norm, axis=-1, keepdims=True)
    )
    grad_mixed = jnp.dot(
        grad_hidden.astype(jnp.bfloat16), out_weight.T, preferred_element_type=jnp.float32
    ).astype(jnp.bfloat16)
    output = jnp.zeros_like(out_sorted).at[positions].set(out_sorted)
    grad_blocks = grad_mixed.reshape(block_count, block_len, local_heads, HD)
    attended_blocks = attended_output.reshape(block_count, block_len, local_heads, HD)
    deltas = jnp.einsum(
        "bqhd,bqhd->bhq", grad_blocks, attended_blocks, preferred_element_type=jnp.float32
    )

    def back_step(slot_pos, carried):
        query_gradient, grad_pair_blocks = carried
        attention_scores, table, key_tile_blocks, value_tile_blocks = slot_scores(slot_pos)
        complete_probabilities = jnp.exp(attention_scores - log_total[..., None])
        probability_gradient = jnp.einsum(
            "bqhd,bkhd->bhqk", grad_blocks, value_tile_blocks, preferred_element_type=jnp.float32
        )
        score_gradient = (
            complete_probabilities * (probability_gradient - deltas[..., None])
        ).astype(jnp.bfloat16)
        query_gradient = (
            query_gradient
            + jnp.einsum(
                "bhqk,bkhd->bqhd",
                score_gradient,
                key_tile_blocks,
                preferred_element_type=jnp.float32,
            )
            * scale_for_scores
        )
        key_portion = (
            jnp.einsum(
                "bhqk,bqhd->bkhd", score_gradient, query_blocks, preferred_element_type=jnp.float32
            )
            * scale_for_scores
        )
        value_portion = jnp.einsum(
            "bhqk,bqhd->bkhd",
            complete_probabilities.astype(jnp.bfloat16),
            grad_blocks,
            preferred_element_type=jnp.float32,
        )
        portion = jnp.concatenate(
            [
                key_portion.reshape(block_count, block_len, col_share),
                value_portion.reshape(block_count, block_len, col_share),
            ],
            axis=2,
        )
        grad_pair_blocks = grad_pair_blocks + jnp.einsum(
            "bc,bkf->ckf", table.astype(jnp.float32), portion, precision=highest_precision
        )
        return (query_gradient, grad_pair_blocks)

    zero_query = jnp.zeros((block_count, block_len, local_heads, HD), jnp.float32)
    zero_wide = jnp.zeros((wide_blocks, block_len, 2 * col_share), jnp.float32)
    query_gradient, grad_pair_blocks = lax.fori_loop(
        0, top_count, back_step, (zero_query, zero_wide)
    )
    grad_pairs = grad_pair_blocks.reshape(wide_rows, 2 * col_share)
    pair_wide = pair_weights.astype(jnp.float32)
    query_part = jnp.dot(
        query_gradient.reshape(row_count, col_share),
        query_weight.astype(jnp.float32).T,
        precision=highest_precision,
    )
    grad_wide = jnp.dot(grad_pairs, pair_wide.T, precision=highest_precision)
    from_right = from_behind(grad_wide[:row_count].astype(jnp.bfloat16), "elem", -1).astype(
        jnp.float32
    )
    from_left = from_behind(grad_wide[2 * row_count :].astype(jnp.bfloat16), "elem", 1).astype(
        jnp.float32
    )
    group_term = query_part + grad_wide[row_count : 2 * row_count] + from_right + from_left
    grad_norm = lax.psum(group_term.astype(jnp.bfloat16), "head").astype(jnp.float32)
    scaled_one = grad_norm * attn_gain
    row_gradients = grad_hidden + first_scale * (
        scaled_one - first_norm * jnp.mean(scaled_one * first_norm, axis=-1, keepdims=True)
    )
    grad_share = lax.dynamic_slice_in_dim(row_gradients, col_start, col_share, 1)
    input_grad = jnp.zeros_like(grad_share).at[positions].set(grad_share)
    return (output, input_grad)


def solution(mesh):
    in_specs = (
        P("elem", None),
        P("elem", None),
        P("elem"),
        P("elem", None),
        P("elem"),
        P(),
        P(None, "head"),
        P(None, "head"),
        P(None, "head"),
        P("head", None),
        P(),
        P(None, "head"),
        P("head", None),
    )
    out_specs = (P("elem", "head"), P("elem", "head"))
    return jax.shard_map(local, mesh=mesh, in_specs=in_specs, out_specs=out_specs, check_vma=False)
```

profile of v0, /device:TPU:0, one launch (start us, length us, event | category | flops | bytes accessed | tf_op | source)
XLA Modules:
  0.0 722.0 jit_solution(11235072406354910245)
XLA Ops:
  48.6 56.0 %while.37 = (s32[]{:T(128)}, f32[8,4,128]{2,1,0:T(4,128)S(1)}, f32[8,4,128]{2,1,0:T(4,128)S(1)}, s32[]{:T(128)}, s32[8]{0:T(128)S(1)}, /*index=5*/s32[8,12]{0,1:...) while((s32[]{:T(128)}, f32[8,4,128]{2,1,0:T(4,128)S(1)}, ...), condition=%wide.region_7.9_spmd.clone, body=%wide.region_4.8_spmd.clone.sunk | while | flops 95953104 | bytes 11747639 | solution.py:122
  105.8 95.0 %while.38 = (s32[]{:T(128)}, f32[8,128,4,64]{1,3,2,0:T(8,128)}, s32[]{:T(128)}, s32[8,12]{0,1:T(8,128)S(1)}, bf16[24,128,512]{2,0,1:T(8,128)(2,1)}, /*index=5*/s...) while((s32[]{:T(128)}, f32[8,128,4,64]{1,3,2,0:T(8,128)}, ...), condition=%wide.region_9.11_spmd.clone, body=%wide.region_8.10_spmd.clone.sunk | while | flops 162267344 | bytes 12075311 | solution.py:132
  209.1 40.8 %all-reduce.5.cloned.1.call-done = bf16[1024,512]{1,0:T(8,128)(2,1)} async-done(((bf16[1024,512]{1,0:T(8,128)(2,1)}), bf16[1024,512]{1,0:T(8,128)(2,1)}) %all-reduce.5.cloned.1.call-update) | async-done | bytes 1048592 | tf_op jit(solution)/shard_map/psum | solution.py:136
  255.6 7.6 %fusion.58 = bf16[1024,512]{1,0:T(8,128)(2,1)} fusion(bf16[512,1024]{1,0:T(8,128)(2,1)S(1)} %copy-done, f32[1024,1024]{1,0:T(8,128)} %fusion.60, bf16[1024,512]{1,0:T(8,128)(2,1)} %param.33, bf16[1024,512]{1,0:T(8,128)(2,1)} %gather_fusion.1, pred[1024]{0:T(1024)(128)(4,1)S(1)} %get-tuple-element.344), kind=kOutput, calls=%fused_computation.94 | convolution fusion | flops 2169503744 | bytes 8389632 | tf_op jit(solution)/shard_map/dot_general | solution.py:158
  263.4 39.9 %all-reduce.7.cloned.1.call-done = bf16[1024,512]{1,0:T(8,128)(2,1)} async-done(((bf16[1024,512]{1,0:T(8,128)(2,1)}), bf16[1024,512]{1,0:T(8,128)(2,1)}) %all-reduce.7.cloned.1.call-update) | async-done | bytes 1048592 | tf_op jit(solution)/shard_map/psum | solution.py:157
  314.5 279.4 %while.39 = (s32[]{:T(128)}, f32[8,128,4,64]{1,3,2,0:T(8,128)}, f32[24,128,512]{2,0,1:T(8,128)}, s32[]{:T(128)}, s32[8,12]{0,1:T(8,128)S(1)}, /*index=5*/bf16[24...) while((s32[]{:T(128)}, f32[8,128,4,64]{1,3,2,0:T(8,128)}, ...), condition=%wide.region_17.19_spmd.clone, body=%wide.region_16.18_spmd.clone.sunk | while | flops 518783360 | bytes 61374988 | solution.py:220
  331.0 6.7 convolution_add_fusion.2
  354.2 6.7 convolution_add_fusion.2
  377.4 6.7 convolution_add_fusion.2
  400.6 6.7 convolution_add_fusion.2
  423.8 6.7 convolution_add_fusion.2
  447.0 6.7 convolution_add_fusion.2
  470.2 6.7 convolution_add_fusion.2
  493.4 6.7 convolution_add_fusion.2
  516.6 6.7 convolution_add_fusion.2
  539.8 6.7 convolution_add_fusion.2
  563.0 6.7 convolution_add_fusion.2
  586.2 6.7 convolution_add_fusion.2
  593.9 6.5 copy.60
  600.4 5.5 fusion.108
  613.8 9.3 %collective-permute-done.3 = bf16[1024,512]{1,0:T(8,128)(2,1)S(1)} collective-permute-done((bf16[1024,512]{1,0:T(8,128)(2,1)S(1)}, bf16[1024,512]{1,0:T(8,128)(2,1)S(1)}, u32[]{:S(2)}, u32[]{:S(2)}) %collective-permute-start.3) | collective-permute-done | bytes 1048608 | tf_op jit(solution)/shard_map/ppermute | solution.py:27
  626.2 71.7 %all-reduce.9.cloned.1.call-done = (bf16[1024,512]{1,0:T(8,128)(2,1)}, bf16[1024,512]{1,0:T(8,128)(2,1)}) async-done(((bf16[1024,512]{1,0:T(8,128)(2,1)}, bf16[1024,512]{1,0:T(8,128)(2,1)}), (bf16[1024,512]{1,0:T(8,128)(2,1)}, bf16[1024,512]{1,0:T(8,128)(2,1)})) %all-reduce.9.cloned.1.call-update) | async-done | bytes 2097168 | tf_op jit(solution)/shard_map/psum | solution.py:149
  701.9 6.1 scatter_custom_fusion
  708.1 7.2 scatter_custom_fusion.1
  (616 shorter events, 405.1 us)
Async XLA Ops:
  7.2 245.0 %copy-start = (bf16[512,1024]{1,0:T(8,128)(2,1)S(1)}, bf16[512,1024]{1,0:T(8,128)(2,1)}, u32[]{:S(2)}) copy-start(bf16[512,1024]{1,0:T(8,128)(2,1)} %param.32) | copy-start | bytes 3145732
  7.2 242.8 %all-reduce.5.cloned.1.call-start = ((), (), s32[]{:S(2)}) async-start(), calls=%async_computation | async-start | bytes 2097152 | tf_op jit(solution)/shard_map/psum | solution.py:136
  8.6 6.0 copy-start.30
  14.0 7.9 %copy-start.13 = (bf16[1024,512]{1,0:T(8,128)(2,1)}, bf16[1024,512]{1,0:T(8,128)(2,1)S(1)}, u32[]{:S(2)}) copy-start(bf16[1024,512]{1,0:T(8,128)(2,1)S(1)} %gather_fusion) | copy-start | bytes 3145732
  14.0 6.6 copy-start.22
  15.2 17.7 %collective-permute-start.1 = (bf16[1024,512]{1,0:T(8,128)(2,1)S(1)}, bf16[1024,512]{1,0:T(8,128)(2,1)}, u32[]{:S(2)}, u32[]{:S(2)}) collective-permute-start(bf16[1024,512]{1,0:T(8,128)(2,1)S(1)} %multiply_convert_fusion.3), channel_id=1, source_target_pairs={{2,0},{4,2},{6,4},{8,6},{10,8},{12,10},{14,12},{16,14},{18,16},{20... | collective-permute-start | bytes 3145736 | tf_op jit(solution)/shard_map/ppermute | solution.py:19
  20.6 17.1 %collective-permute-start = (bf16[1024,512]{1,0:T(8,128)(2,1)S(1)}, bf16[1024,512]{1,0:T(8,128)(2,1)}, u32[]{:S(2)}, u32[]{:S(2)}) collective-permute-start(bf16[1024,512]{1,0:T(8,128)(2,1)S(1)} %multiply_convert_fusion.3), channel_id=1, source_target_pairs={{0,2},{2,4},{4,6},{6,8},{8,10},{10,12},{12,14},{14,16},{16,18},{18... | collective-permute-start | bytes 3145736 | tf_op jit(solution)/shard_map/ppermute | solution.py:16
  28.5 12.6 %copy-start.20 = (bf16[512,512]{1,0:T(8,128)(2,1)}, bf16[512,512]{1,0:T(8,128)(2,1)S(1)}, u32[]{:S(2)}) copy-start(bf16[512,512]{1,0:T(8,128)(2,1)S(1)} %constant_dynamic-update-slice_fusion) | copy-start | bytes 1572868
  204.0 99.3 %all-reduce.7.cloned.1.call-start = ((), (), s32[]{:S(2)}) async-start(), calls=%async_computation.1 | async-start | bytes 2097152 | tf_op jit(solution)/shard_map/psum | solution.py:157
  209.1 43.1 %copy-start.28 = (f32[512]{0:T(512)S(1)}, f32[512]{0:T(512)}, u32[]{:S(2)}) copy-start(f32[512]{0:T(512)} %param.31) | copy-start | bytes 6148
  252.2 53.0 %copy-start.7 = (f32[1024,512]{1,0:T(8,128)}, f32[1024,512]{1,0:T(8,128)S(1)}, u32[]{:S(2)}) copy-start(f32[1024,512]{1,0:T(8,128)S(1)} %get-tuple-element.343) | copy-start | bytes 6291460
  263.1 42.1 %copy-start.18 = (bf16[1024,512]{1,0:T(8,128)(2,1)S(1)}, bf16[1024,512]{1,0:T(8,128)(2,1)}, u32[]{:S(2)}) copy-start(bf16[1024,512]{1,0:T(8,128)(2,1)} %gather_fusion.1) | copy-start | bytes 3145732
  263.1 434.8 %all-reduce.9.cloned.1.call-start = ((), (), s32[]{:S(2)}) async-start(), calls=%async_computation.2 | async-start | bytes 4194304 | tf_op jit(solution)/shard_map/psum | solution.py:149
  593.9 6.5 copy-start.21
  600.4 10.3 %copy-start.33 = (bf16[1024,512]{1,0:T(8,128)(2,1)S(1)}, bf16[1024,512]{1,0:T(8,128)(2,1)}, u32[]{:S(2)}) copy-start(bf16[1024,512]{1,0:T(8,128)(2,1)} %param.33) | copy-start | bytes 3145732
  605.9 4.8 copy-start.16
  606.1 17.1 %collective-permute-start.3 = (bf16[1024,512]{1,0:T(8,128)(2,1)S(1)}, bf16[1024,512]{1,0:T(8,128)(2,1)S(1)}, u32[]{:S(2)}, u32[]{:S(2)}) collective-permute-start(bf16[1024,512]{1,0:T(8,128)(2,1)S(1)} %get-tuple-element.353), channel_id=1, source_target_pairs={{0,2},{2,4},{4,6},{6,8},{8,10},{10,12},{12,14},{14,16},{16,18},{18... | collective-permute-start | bytes 3145736 | tf_op jit(solution)/shard_map/ppermute | solution.py:27
  606.1 7.1 copy-start.12
  606.2 17.0 %collective-permute-start.2 = (bf16[1024,512]{1,0:T(8,128)(2,1)S(1)}, bf16[1024,512]{1,0:T(8,128)(2,1)S(1)}, u32[]{:S(2)}, u32[]{:S(2)}) collective-permute-start(bf16[1024,512]{1,0:T(8,128)(2,1)S(1)} %get-tuple-element.352), channel_id=1, source_target_pairs={{0,30},{2,0},{4,2},{6,4},{8,6},{10,8},{12,10},{14,12},{16,14},{18,... | collective-permute-start | bytes 3145736 | tf_op jit(solution)/shard_map/ppermute | solution.py:27
  613.2 10.0 %copy-start.23 = (bf16[512,256]{1,0:T(8,128)(2,1)S(1)}, bf16[512,256]{1,0:T(8,128)(2,1)}, u32[]{:S(2)}) copy-start(bf16[512,256]{1,0:T(8,128)(2,1)} %param.27) | copy-start | bytes 786436
  626.2 71.7 %copy-start.14 = (bf16[1024,512]{1,0:T(8,128)(2,1)S(1)}, bf16[1024,512]{1,0:T(8,128)(2,1)}, u32[]{:S(2)}) copy-start(bf16[1024,512]{1,0:T(8,128)(2,1)} %copy-done.13) | copy-start | bytes 3145732
  626.2 71.7 %copy-start.27 = (f32[1024]{0:T(1024)S(1)}, f32[1024]{0:T(1024)}, u32[]{:S(2)}) copy-start(f32[1024]{0:T(1024)} %copy-done.26) | copy-start | bytes 12292
  626.2 71.7 %copy-start.31 = (f32[512]{0:T(512)S(1)}, f32[512]{0:T(512)}, u32[]{:S(2)}) copy-start(f32[512]{0:T(512)} %param.26) | copy-start | bytes 6148
  708.1 7.2 copy-start.1
  (84 other events, 177.2 us)
Sparse Core Ops, SparseCore 0:
  204.1 45.7 all-reduce.4
  263.3 40.0 all-reduce.6
  626.4 71.5 all-reduce.8
where the time goes:
time: 734 us; the launch traced here: 722 us
  matrix products  348 us (47%)
  waiting for transfers between devices  171 us (23%)
  local copies, waits for them, and re-layouts  117 us (16%)
  other arithmetic  33.7 us (5%)
  loops' own time  27.3 us (4%)
  between operations  14.4 us (2%)
  starting transfers between devices  10.4 us (1%)
    dot_general x36, matrix products, slot_scores(): jnp.einsum('bc,ckf->bkf', table.astype(jnp.bfloat16), pair_blocks, prefer...  91.6 us
    dot_general x12, matrix products, back_step(): jnp.einsum('bc,bkf->ckf', table.astype(jnp.float32), portion, precision=h...  80.6 us
    psum x1, waiting for transfers between devices, local(): lax.psum(ffn_terms.astype(jnp.bfloat16), 'head').astype(jnp.float32)  71.7 us
    dot_general x12, matrix products, output_step(): jnp.einsum('bhqk,bkhd->bqhd', attn_probs, value_tile_blocks, preferred_el...  44.3 us
    psum x1, waiting for transfers between devices, local(): lax.psum(jnp.dot(attended_output, out_weight, preferred_element_type=jnp....  40.8 us
    psum x1, waiting for transfers between devices, local(): lax.psum(jnp.dot(grad_pre, ffn_in.T, preferred_element_type=jnp.float32)....  39.9 us
    dot_general x24, matrix products, slot_scores(): jnp.einsum('bqhd,bkhd->bhqk', query_blocks, key_tile_blocks, preferred_el...  32.1 us
    slice x36, local copies, waits for them, and re-layouts, slot_scores(): tiles[:, :, col_share:].reshape(block_count, block_len, local_heads, HD)  29.8 us
  transfers between devices with their start and end apart: 7, of which 6 were waited for; matrix products, arithmetic and copies ran while one was open for 2% of the time, Pallas kernels for 0%

commit v1 on v0

--- a/solution.py
+++ b/solution.py
@@ -133,11 +133,14 @@
         0, top_count, output_step, jnp.zeros((block_count, block_len, local_heads, HD), jnp.float32)
     )
     attended_output = attended_sum.reshape(row_count, col_share).astype(jnp.bfloat16)
-    mixed_heads = lax.psum(
-        jnp.dot(attended_output, out_weight, preferred_element_type=jnp.float32).astype(
-            jnp.bfloat16
+    mixed_heads = jnp.sum(
+        lax.all_gather(
+            jnp.dot(attended_output, out_weight, preferred_element_type=jnp.float32).astype(
+                jnp.bfloat16
+            ),
+            "head",
         ),
-        "head",
+        axis=0,
     ).astype(jnp.float32)
     hidden_in = ordered_rows + mixed_heads
     second_scale = row_scale(hidden_in)

time: 734 us -> 731 us (level)
    psum x1 -> x0, waiting for transfers between devices: 40.8 us -> none  [local(): lax.psum(jnp.dot(attended_output, out_weight, preferred_element_type=jnp....]
    all_gather x0 -> x1, waiting for transfers between devices: none -> 33.7 us  [local(): lax.all_gather(jnp.dot(attended_output, out_weight, preferred_element_typ...]
where the time goes in v1:
time: 731 us; the launch traced here: 719 us
  matrix products  348 us (48%)
  waiting for transfers between devices  164 us (22%)
  local copies, waits for them, and re-layouts  117 us (16%)
  other arithmetic  37 us (5%)
  loops' own time  27.7 us (4%)
  between operations  14.7 us (2%)
  starting transfers between devices  10.5 us (1%)
    dot_general x36, matrix products, slot_scores(): jnp.einsum('bc,ckf->bkf', table.astype(jnp.bfloat16), pair_blocks, prefer...  91.6 us
    dot_general x12, matrix products, back_step(): jnp.einsum('bc,bkf->ckf', table.astype(jnp.float32), portion, precision=h...  80.6 us
    psum x1, waiting for transfers between devices, local(): lax.psum(ffn_terms.astype(jnp.bfloat16), 'head').astype(jnp.float32)  71.7 us
    dot_general x12, matrix products, output_step(): jnp.einsum('bhqk,bkhd->bqhd', attn_probs, value_tile_blocks, preferred_el...  44.3 us
    psum x1, waiting for transfers between devices, local(): lax.psum(jnp.dot(grad_pre, ffn_in.T, preferred_element_type=jnp.float32)....  40.2 us
    all_gather x1, waiting for transfers between devices, local(): lax.all_gather(jnp.dot(attended_output, out_weight, preferred_element_typ...  33.7 us
    dot_general x24, matrix products, slot_scores(): jnp.einsum('bqhd,bkhd->bhqk', query_blocks, key_tile_blocks, preferred_el...  32.1 us
    slice x36, local copies, waits for them, and re-layouts, slot_scores(): tiles[:, :, col_share:].reshape(block_count, block_len, local_heads, HD)  29.8 us
  transfers between devices with their start and end apart: 7, of which 6 were waited for; matrix products, arithmetic and copies ran while one was open for 2% of the time, Pallas kernels for 0%

profile of v1, /device:TPU:0, one launch (start us, length us, event | category | flops | bytes accessed | tf_op | source)
XLA Modules:
  0.0 719.1 jit_solution(14757700686750057754)
XLA Ops:
  48.6 56.4 %while.37 = (s32[]{:T(128)}, f32[8,4,128]{2,1,0:T(4,128)S(1)}, f32[8,4,128]{2,1,0:T(4,128)S(1)}, s32[]{:T(128)}, s32[8]{0:T(128)S(1)}, /*index=5*/s32[8,12]{0,1:...) while((s32[]{:T(128)}, f32[8,4,128]{2,1,0:T(4,128)S(1)}, ...), condition=%wide.region_7.9_spmd.clone, body=%wide.region_4.8_spmd.clone.sunk | while | flops 95953104 | bytes 11747639 | solution.py:122
  106.1 95.0 %while.38 = (s32[]{:T(128)}, f32[8,128,4,64]{1,3,2,0:T(8,128)}, s32[]{:T(128)}, s32[8,12]{0,1:T(8,128)S(1)}, bf16[24,128,512]{2,0,1:T(8,128)(2,1)}, /*index=5*/s...) while((s32[]{:T(128)}, f32[8,128,4,64]{1,3,2,0:T(8,128)}, ...), condition=%wide.region_9.11_spmd.clone, body=%wide.region_8.10_spmd.clone.sunk | while | flops 162267344 | bytes 12075311 | solution.py:132
  209.7 33.7 %all-gather.3.cloned.1.call-done = bf16[2048,512]{1,0:T(8,128)(2,1)} async-done(((bf16[1024,512]{1,0:T(8,128)(2,1)}), bf16[2048,512]{1,0:T(8,128)(2,1)}) %all-gather.3.cloned.1.call-update) | async-done | bytes 2097168 | tf_op jit(solution)/shard_map/all_gather | solution.py:137
  252.2 7.6 %fusion.58 = bf16[1024,512]{1,0:T(8,128)(2,1)} fusion(bf16[512,1024]{1,0:T(8,128)(2,1)S(1)} %copy-done, f32[1024,1024]{1,0:T(8,128)} %fusion.60, bf16[1024,512]{1,0:T(8,128)(2,1)} %param.33, bf16[1024,512]{1,0:T(8,128)(2,1)} %gather_fusion.1, pred[1024]{0:T(1024)(128)(4,1)S(1)} %get-tuple-element.344), kind=kOutput, calls=%fused_computation.94 | convolution fusion | flops 2169503744 | bytes 8389632 | tf_op jit(solution)/shard_map/dot_general | solution.py:161
  259.9 40.2 %all-reduce.4.cloned.1.call-done = bf16[1024,512]{1,0:T(8,128)(2,1)} async-done(((bf16[1024,512]{1,0:T(8,128)(2,1)}), bf16[1024,512]{1,0:T(8,128)(2,1)}) %all-reduce.4.cloned.1.call-update) | async-done | bytes 1048592 | tf_op jit(solution)/shard_map/psum | solution.py:160
  311.2 279.5 %while.39 = (s32[]{:T(128)}, f32[8,128,4,64]{1,3,2,0:T(8,128)}, f32[24,128,512]{2,0,1:T(8,128)}, s32[]{:T(128)}, s32[8,12]{0,1:T(8,128)S(1)}, /*index=5*/bf16[24...) while((s32[]{:T(128)}, f32[8,128,4,64]{1,3,2,0:T(8,128)}, ...), condition=%wide.region_17.19_spmd.clone, body=%wide.region_16.18_spmd.clone.sunk | while | flops 518783360 | bytes 61374988 | solution.py:223
  327.9 6.7 convolution_add_fusion.2
  351.1 6.7 convolution_add_fusion.2
  374.3 6.7 convolution_add_fusion.2
  397.5 6.7 convolution_add_fusion.2
  420.7 6.7 convolution_add_fusion.2
  443.9 6.7 convolution_add_fusion.2
  467.1 6.7 convolution_add_fusion.2
  490.3 6.7 convolution_add_fusion.2
  513.5 6.7 convolution_add_fusion.2
  536.7 6.7 convolution_add_fusion.2
  559.9 6.7 convolution_add_fusion.2
  583.1 6.7 convolution_add_fusion.2
  590.7 6.5 copy.60
  597.2 5.5 fusion.108
  610.7 9.2 %collective-permute-done.3 = bf16[1024,512]{1,0:T(8,128)(2,1)S(1)} collective-permute-done((bf16[1024,512]{1,0:T(8,128)(2,1)S(1)}, bf16[1024,512]{1,0:T(8,128)(2,1)S(1)}, u32[]{:S(2)}, u32[]{:S(2)}) %collective-permute-start.3) | collective-permute-done | bytes 1048608 | tf_op jit(solution)/shard_map/ppermute | solution.py:27
  623.0 71.7 %all-reduce.6.cloned.1.call-done = (bf16[1024,512]{1,0:T(8,128)(2,1)}, bf16[1024,512]{1,0:T(8,128)(2,1)}) async-done(((bf16[1024,512]{1,0:T(8,128)(2,1)}, bf16[1024,512]{1,0:T(8,128)(2,1)}), (bf16[1024,512]{1,0:T(8,128)(2,1)}, bf16[1024,512]{1,0:T(8,128)(2,1)})) %all-reduce.6.cloned.1.call-update) | async-done | bytes 2097168 | tf_op jit(solution)/shard_map/psum | solution.py:152
  698.7 6.1 scatter_custom_fusion
  704.9 7.2 scatter_custom_fusion.1
  (617 shorter events, 408.5 us)
Async XLA Ops:
  7.2 241.7 %copy-start = (bf16[512,1024]{1,0:T(8,128)(2,1)S(1)}, bf16[512,1024]{1,0:T(8,128)(2,1)}, u32[]{:S(2)}) copy-start(bf16[512,1024]{1,0:T(8,128)(2,1)} %param.32) | copy-start | bytes 3145732
  7.2 236.2 %all-gather.3.cloned.1.call-start = ((), (), s32[]{:S(2)}) async-start(), calls=%async_computation.1 | async-start | bytes 3145728 | tf_op jit(solution)/shard_map/all_gather | solution.py:137
  8.6 6.0 copy-start.30
  14.0 7.9 %copy-start.13 = (bf16[1024,512]{1,0:T(8,128)(2,1)}, bf16[1024,512]{1,0:T(8,128)(2,1)S(1)}, u32[]{:S(2)}) copy-start(bf16[1024,512]{1,0:T(8,128)(2,1)S(1)} %gather_fusion) | copy-start | bytes 3145732
  14.0 6.6 copy-start.22
  15.2 17.7 %collective-permute-start.1 = (bf16[1024,512]{1,0:T(8,128)(2,1)S(1)}, bf16[1024,512]{1,0:T(8,128)(2,1)}, u32[]{:S(2)}, u32[]{:S(2)}) collective-permute-start(bf16[1024,512]{1,0:T(8,128)(2,1)S(1)} %multiply_convert_fusion.3), channel_id=1, source_target_pairs={{2,0},{4,2},{6,4},{8,6},{10,8},{12,10},{14,12},{16,14},{18,16},{20... | collective-permute-start | bytes 3145736 | tf_op jit(solution)/shard_map/ppermute | solution.py:19
  20.6 17.1 %collective-permute-start = (bf16[1024,512]{1,0:T(8,128)(2,1)S(1)}, bf16[1024,512]{1,0:T(8,128)(2,1)}, u32[]{:S(2)}, u32[]{:S(2)}) collective-permute-start(bf16[1024,512]{1,0:T(8,128)(2,1)S(1)} %multiply_convert_fusion.3), channel_id=1, source_target_pairs={{0,2},{2,4},{4,6},{6,8},{8,10},{10,12},{12,14},{14,16},{16,18},{18... | collective-permute-start | bytes 3145736 | tf_op jit(solution)/shard_map/ppermute | solution.py:16
  28.5 12.6 %copy-start.20 = (bf16[512,512]{1,0:T(8,128)(2,1)}, bf16[512,512]{1,0:T(8,128)(2,1)S(1)}, u32[]{:S(2)}) copy-start(bf16[512,512]{1,0:T(8,128)(2,1)S(1)} %constant_dynamic-update-slice_fusion) | copy-start | bytes 1572868
  204.4 95.7 %all-reduce.4.cloned.1.call-start = ((), (), s32[]{:S(2)}) async-start(), calls=%async_computation | async-start | bytes 2097152 | tf_op jit(solution)/shard_map/psum | solution.py:160
  248.9 53.0 %copy-start.7 = (f32[1024,512]{1,0:T(8,128)}, f32[1024,512]{1,0:T(8,128)S(1)}, u32[]{:S(2)}) copy-start(f32[1024,512]{1,0:T(8,128)S(1)} %get-tuple-element.343) | copy-start | bytes 6291460
  259.8 42.1 %copy-start.18 = (bf16[1024,512]{1,0:T(8,128)(2,1)S(1)}, bf16[1024,512]{1,0:T(8,128)(2,1)}, u32[]{:S(2)}) copy-start(bf16[1024,512]{1,0:T(8,128)(2,1)} %gather_fusion.1) | copy-start | bytes 3145732
  259.8 434.9 %all-reduce.6.cloned.1.call-start = ((), (), s32[]{:S(2)}) async-start(), calls=%async_computation.2 | async-start | bytes 4194304 | tf_op jit(solution)/shard_map/psum | solution.py:152
  590.7 6.5 copy-start.21
  597.2 10.4 %copy-start.33 = (bf16[1024,512]{1,0:T(8,128)(2,1)S(1)}, bf16[1024,512]{1,0:T(8,128)(2,1)}, u32[]{:S(2)}) copy-start(bf16[1024,512]{1,0:T(8,128)(2,1)} %param.33) | copy-start | bytes 3145732
  602.7 4.9 copy-start.16
  602.8 17.1 %collective-permute-start.3 = (bf16[1024,512]{1,0:T(8,128)(2,1)S(1)}, bf16[1024,512]{1,0:T(8,128)(2,1)S(1)}, u32[]{:S(2)}, u32[]{:S(2)}) collective-permute-start(bf16[1024,512]{1,0:T(8,128)(2,1)S(1)} %get-tuple-element.353), channel_id=1, source_target_pairs={{0,2},{2,4},{4,6},{6,8},{8,10},{10,12},{12,14},{14,16},{16,18},{18... | collective-permute-start | bytes 3145736 | tf_op jit(solution)/shard_map/ppermute | solution.py:27
  602.9 7.2 copy-start.12
  602.9 17.0 %collective-permute-start.2 = (bf16[1024,512]{1,0:T(8,128)(2,1)S(1)}, bf16[1024,512]{1,0:T(8,128)(2,1)S(1)}, u32[]{:S(2)}, u32[]{:S(2)}) collective-permute-start(bf16[1024,512]{1,0:T(8,128)(2,1)S(1)} %get-tuple-element.352), channel_id=1, source_target_pairs={{0,30},{2,0},{4,2},{6,4},{8,6},{10,8},{12,10},{14,12},{16,14},{18,... | collective-permute-start | bytes 3145736 | tf_op jit(solution)/shard_map/ppermute | solution.py:27
  610.1 9.8 %copy-start.23 = (bf16[512,256]{1,0:T(8,128)(2,1)S(1)}, bf16[512,256]{1,0:T(8,128)(2,1)}, u32[]{:S(2)}) copy-start(bf16[512,256]{1,0:T(8,128)(2,1)} %param.27) | copy-start | bytes 786436
  623.0 71.7 %copy-start.14 = (bf16[1024,512]{1,0:T(8,128)(2,1)S(1)}, bf16[1024,512]{1,0:T(8,128)(2,1)}, u32[]{:S(2)}) copy-start(bf16[1024,512]{1,0:T(8,128)(2,1)} %copy-done.13) | copy-start | bytes 3145732
  623.0 71.7 %copy-start.27 = (f32[1024]{0:T(1024)S(1)}, f32[1024]{0:T(1024)}, u32[]{:S(2)}) copy-start(f32[1024]{0:T(1024)} %copy-done.26) | copy-start | bytes 12292
  623.0 71.7 %copy-start.31 = (f32[512]{0:T(512)S(1)}, f32[512]{0:T(512)}, u32[]{:S(2)}) copy-start(f32[512]{0:T(512)} %param.26) | copy-start | bytes 6148
  694.7 4.0 copy-start.8
  704.9 7.2 copy-start.1
  (84 other events, 175.6 us)
Sparse Core Ops, SparseCore 0:
  204.5 38.8 all-gather.2
  259.9 40.0 all-reduce.3
  623.1 71.5 all-reduce.5
